TPU v7x, 32 devices: a whole 2x2x4 slice. The times are simulated.
32 devices in a mesh: dp: 4 (over y, x), mp: 8 (over z, core).
Axes of the slice: x: 2, y: 2, z: 4, core: 2. Of those that a mesh axis runs over, the one named last changes fastest.
Arguments:
- train_acts: bfloat16 [512, 4096], P('dp', 'mp'), may hold values from -6 to 6
- train_grads: bfloat16 [512, 7168], P('dp', 'mp'), may hold values from -0.75 to 0.75
- query_acts: bfloat16 [1024, 4096], P('dp', 'mp'), may hold values from -6 to 6
- query_grads: bfloat16 [1024, 7168], P('dp', 'mp'), may hold values from -0.75 to 0.75
- basis_in: bfloat16 [4096, 4096], P('mp'), may hold values from -0.125 to 0.125
- basis_out: bfloat16 [7168, 7168], P('mp'), may hold values from -0.09375 to 0.09375
- eigvals: bfloat16 [4096, 7168], P(None, 'mp'), may hold values from 0.25 to 4
Outputs:
- scores: float32 [16, 8], P(None, 'dp')
- energies: float32 [8], P('dp')
All inputs are finite; a program needn't handle non-finite values.
Results may differ from a plain program's by a relative error of at most 0.0048.
Values may be sent and summed in bfloat16 or wider, within the bound.
No kernel may reach another device: no remote copies, remote signals or barrier semaphores. Data moves between devices by JAX's collectives and lax.ppermute only.
A program may use at most 128 MiB of HBM per device.

v0:
```python
import math

import jax
import jax.numpy as jnp
from jax import lax
from jax.sharding import PartitionSpec as P

D = 4096
H = 7168
SEQ = 64


damping = 0.1


def pair_scores(query_a, query_g, scaled):
    applied = jnp.einsum("it,nij->ntj", query_a, scaled, preferred_element_type=jnp.float32)
    per_token = jnp.sum(applied * jnp.transpose(query_g).astype(jnp.float32)[None], axis=2)
    grouped = jnp.sum(per_token.reshape(per_token.shape[0], -1, SEQ), axis=2)
    return jnp.transpose(grouped)


def on_device(train_acts, train_grads, query_acts, query_grads, basis_in, basis_out, eigvals):
    train_rows = train_acts.shape[0]
    train_seqs = train_rows // SEQ
    acts = jnp.concatenate([train_acts, query_acts], axis=0)
    grads = jnp.concatenate([train_grads, query_grads], axis=0)
    columns = basis_in
    rot_acts = lax.psum(
        jnp.einsum("fc,rf->cr", columns, acts, preferred_element_type=jnp.float32), "mp"
    ).astype(jnp.bfloat16)
    columns = basis_out
    rot_grads = lax.psum_scatter(
        jnp.einsum("fc,rf->cr", columns, grads, preferred_element_type=jnp.float32),
        "mp",
        scatter_dimension=0,
        tiled=True,
    ).astype(jnp.bfloat16)
    train_a = rot_acts[:, :train_rows].reshape(rot_acts.shape[0], train_seqs, SEQ)
    train_g = rot_grads[:, :train_rows].reshape(rot_grads.shape[0], train_seqs, SEQ)
    query_a = rot_acts[:, train_rows:]
    query_g = rot_grads[:, train_rows:]
    train_outer = jnp.einsum("isk,jsk->sij", train_a, train_g, preferred_element_type=jnp.float32)
    shifted = eigvals.astype(jnp.float32) + damping
    scaled = (train_outer / shifted).astype(jnp.bfloat16)
    energy_part = jnp.sum(train_outer * train_outer, axis=(1, 2))
    all_query_a, all_query_g = (
        lax.all_gather(query_a, "dp", axis=1, tiled=True),
        lax.all_gather(query_g, "dp", axis=1, tiled=True),
    )
    partial_value = pair_scores(all_query_a, all_query_g, scaled)
    total_scores, total_energy = lax.psum((partial_value, energy_part), "mp")
    scores = total_scores * (1.0 / math.sqrt(D * H))
    energies = total_energy / (D * H)
    return (scores, energies)


def solution(mesh):
    return jax.shard_map(
        on_device,
        mesh=mesh,
        in_specs=(
            P("dp", "mp"),
            P("dp", "mp"),
            P("dp", "mp"),
            P("dp", "mp"),
            P("mp", None),
            P("mp", None),
            P(None, "mp"),
        ),
        out_specs=(P(None, "dp"), P("dp")),
        check_vma=False,
    )
```

profile of v0, /device:TPU:0, one launch (start us, length us, event | category | flops | bytes accessed | tf_op | source)
XLA Modules:
  0.0 401.3 jit_solution(1922817455804115351)
XLA Ops:
  7.2 0.0 reduce-scatter.2.cloned.1.call-start
  7.2 11.4 %convolution_bitcast_fusion = f32[7168,384]{0,1:T(8,128)} fusion(bf16[896,7168]{1,0:T(8,128)(2,1)} %param.12, bf16[256,896]{1,0:T(8,128)(2,1)} %param.10, bf16[128,896]{1,0:T(8,128)(2,1)} %param.8), kind=kOutput, calls=%fused_computation.4 | convolution fusion | flops 4933877760 | bytes 24543232 | tf_op jit(solution)/shard_map/fc,rf->cr/dot_general | solution.py:34
  18.7 0.0 copy-start.1
  18.7 0.0 copy-start.2
  18.7 0.0 reduce-scatter.2.cloned.1.call-update
  18.7 0.0 all-gather.5.cloned.1.call-start
  18.7 0.9 copy-done.1
  19.6 0.0 copy-done.2
  19.6 6.6 %convolution_bitcast_fusion.1 = f32[4096,384]{0,1:T(8,128)} fusion(bf16[512,4096]{1,0:T(8,128)(2,1)} %param.11, bf16[256,512]{1,0:T(8,128)(2,1)S(1)} %copy-done.1, bf16[128,512]{1,0:T(8,128)(2,1)S(1)} %copy-done.2), kind=kOutput, calls=%fused_computation.8 | convolution fusion | flops 1611399168 | bytes 10878976 | tf_op jit(solution)/shard_map/fc,rf->cr/dot_general | solution.py:30
  26.2 109.6 %reduce-scatter.2.cloned.1.call-done = f32[896,384]{0,1:T(8,128)} async-done(((f32[7168,384]{0,1:T(8,128)}), f32[896,384]{0,1:T(8,128)}) %reduce-scatter.2.cloned.1.call-update) | async-done | bytes 1376272 | tf_op jit(solution)/shard_map/reduce_scatter | solution.py:33
  135.8 1.4 convert_element_type.19
  137.3 0.0 copy-start
  137.3 0.8 copy-done
  138.1 0.8 slice.19
  138.9 0.0 all-gather.5.cloned.1.call-update
  138.9 0.0 all-gather.3.cloned.1.call-start
  139.0 127.1 %all-reduce.2 = bf16[4096,384]{0,1:T(8,128)(2,1)S(1)} all-reduce(f32[4096,384]{0,1:T(8,128)} %convolution_bitcast_fusion.1), channel_id=1, replica_groups=mesh['dp'=4,'mp'=8] {'mp'}, use_global_device_ids=true, to_apply=%region_0.0 | all-reduce | flops 1572864 | bytes 9437184 | tf_op jit(solution)/shard_map/psum | solution.py:29
  266.1 1.5 slice.18
  267.5 0.0 all-gather.3.cloned.1.call-update
  267.6 0.1 slice.16
  267.6 0.0 slice-start
  267.7 11.2 %convert_add_fusion = f32[4096,896]{1,0:T(8,128)} fusion(bf16[4096,896]{1,0:T(8,128)(2,1)} %param.13), kind=kLoop, calls=%fused_computation.2 | loop fusion | flops 7340032 | bytes 22020096 | tf_op jit(solution)/shard_map/add | solution.py:44
  278.8 0.0 slice-done
  278.8 12.1 %multiply_reduce_fusion = (f32[2]{0:T(128)S(1)}, f32[2,4096,896]{2,1,0:T(8,128)}) fusion(bf16[4096,2,64]{0,2,1:T(8,128)(2,1)S(1)} %bitcast.22, bf16[896,2,64]{0,2,1:T(8,128)(2,1)S(1)} %bitcast.23), kind=kOutput, calls=%fused_computation | convolution fusion | flops 954204160 | bytes 30638088 | tf_op jit(solution)/shard_map/isk,jsk->sij/dot_general | solution.py:43
  290.9 0.0 all-gather.5.cloned.1.call-done
  290.9 3.6 convert_bitcast_fusion
  294.5 5.0 %copy.14 = f32[1024,896]{0,1:T(8,128)} copy(f32[1024,896]{1,0:T(8,128)} %convert_bitcast_fusion) | data formatting | bytes 7340032 | tf_op jit(solution)/shard_map/convert_element_type | solution.py:18
  299.5 54.0 %all-gather.3.cloned.1.call-done = bf16[4096,1024]{0,1:T(8,128)(2,1)} async-done(((bf16[4096,256]{0,1:T(8,128)(2,1)}), bf16[4096,1024]{0,1:T(8,128)(2,1)}) %all-gather.3.cloned.1.call-update) | async-done | bytes 8388624 | tf_op jit(solution)/shard_map/all_gather | solution.py:48
  353.5 23.9 %fusion.2 = f32[2,1024]{1,0:T(2,128)S(1)} fusion(f32[1024,896]{0,1:T(8,128)} %copy.14, bf16[4096,1024]{0,1:T(8,128)(2,1)} %all-gather.3.cloned.1.call-done, f32[2,4096,896]{2,1,0:T(8,128)} %get-tuple-element.5, f32[4096,896]{1,0:T(8,128)} %convert_add_fusion), kind=kOutput, calls=%fused_computation.7 | convolution fusion | flops 15050733568 | bytes 56107008 | tf_op jit(solution)/shard_map/it,nij->ntj/dot_general | solution.py:17
  377.4 0.1 reshape.17
  377.5 0.1 reduce_sum.28
  377.6 16.2 %all-reduce = (f32[16,2]{0,1:T(2,128)S(1)}, f32[2]{0:T(128)S(1)}) all-reduce(f32[16,2]{0,1:T(2,128)S(1)} %bitcast.24, f32[2]{0:T(128)S(1)} %get-tuple-element.4), channel_id=1, replica_groups=mesh['dp'=4,'mp'=8] {'mp'}, use_global_device_ids=true, to_apply=%region_4.0 | all-reduce | flops 34 | bytes 272 | tf_op jit(solution)/shard_map/psum | solution.py:52
  393.7 0.6 broadcast_multiply_fusion
  394.3 0.5 broadcast_multiply_fusion.1
Async XLA Ops:
  7.2 128.7 %reduce-scatter.2.cloned.1.call-start = ((), (), s32[]{:S(2)}) async-start(), calls=%async_computation.1 | async-start | bytes 12386304 | tf_op jit(solution)/shard_map/reduce_scatter | solution.py:33
  18.7 0.9 copy-start.1
  18.7 1.0 copy-start.2
  18.7 272.2 %all-gather.5.cloned.1.call-start = ((), (), s32[]{:S(2)}) async-start(), calls=%async_computation.3 | async-start | bytes 2293760 | tf_op jit(solution)/shard_map/all_gather | solution.py:49
  137.3 0.9 copy-start
  138.9 214.6 %all-gather.3.cloned.1.call-start = ((), (), s32[]{:S(2)}) async-start(), calls=%async_computation.2 | async-start | bytes 10485760 | tf_op jit(solution)/shard_map/all_gather | solution.py:48
  267.6 11.2 %slice-start = ((bf16[896,384]{0,1:T(8,128)(2,1)}), bf16[896,128]{0,1:T(8,128)(2,1)S(1)}, s32[]{:S(2)}) async-start(bf16[896,384]{0,1:T(8,128)(2,1)} %copy-done), calls=%async_computation.4 | async-start | bytes 458752 | tf_op jit(solution)/shard_map/slice | solution.py:40
Sparse Core Ops, SparseCore 0:
  18.8 117.0 reduce-scatter.1
  139.1 31.4 all-gather.4
  267.7 85.7 all-gather.2
where the time goes:
time: 402 us; the launch traced here: 401 us
  waiting for transfers between devices  164 us (41%)
  blocking collectives  143 us (36%)
  matrix products  53.9 us (13%)
  other arithmetic  17.3 us (4%)
  between operations  13.8 us (3%)
  local copies, waits for them, and re-layouts  9.22 us (2%)
    psum x1, blocking collectives, on_device(): lax.psum(jnp.einsum('fc,rf->cr', columns, acts, preferred_element_type=jn...  127 us
    reduce_scatter x1, waiting for transfers between devices, on_device(): lax.psum_scatter(jnp.einsum('fc,rf->cr', columns, grads, preferred_elemen...  110 us
    all_gather x1, waiting for transfers between devices, on_device(): lax.all_gather(query_a, 'dp', axis=1, tiled=True)  54 us
    dot_general x1, matrix products, pair_scores(): jnp.einsum('it,nij->ntj', query_a, scaled, preferred_element_type=jnp.flo...  23.9 us
    psum x1, blocking collectives, on_device(): total_scores, total_energy = lax.psum((partial_value, energy_part), 'mp')  16.2 us
    dot_general x1, matrix products, on_device(): jnp.einsum('isk,jsk->sij', train_a, train_g, preferred_element_type=jnp.f...  12.1 us
    dot_general x1, matrix products, on_device(): jnp.einsum('fc,rf->cr', columns, grads, preferred_element_type=jnp.float32)  11.4 us
    add x1, other arithmetic, on_device(): shifted = eigvals.astype(jnp.float32) + damping  11.2 us
  transfers between devices with their start and end apart: 3, of which 2 were waited for; matrix products, arithmetic and copies ran while one was open for 10% of the time, Pallas kernels for 0%

commit v1 on v0

v1 whole, which is shorter than its diff:
```python
import functools
import math

import jax
import jax.numpy as jnp
from jax import lax
from jax.experimental import pallas as pl
from jax.experimental.pallas import tpu as pltpu
from jax.sharding import PartitionSpec as P

SEQ = 64
LANES = 128

damping = 0.1

ACTS_MAX, BASIS_IN_MAX = 6.0, 0.125
GRADS_MAX, BASIS_OUT_MAX = 0.75, 0.09375

Q_CHUNKS = 2


def gain_of(bound):
    return 2.0 ** math.floor(math.log2(65000.0**2 / bound))


def encode(value, gain):
    root = jnp.sqrt(jnp.abs(value) * gain)
    return jnp.where(value < 0, -root, root).astype(jnp.float16)


def decode(coded, gain):
    root = coded.astype(jnp.float32)
    return root * jnp.abs(root) * (1.0 / gain)


def reversed_bits(p, bits):
    out = 0
    for b in range(bits):
        out |= ((p >> b) & 1) << (bits - 1 - b)
    return out


def swap(x, axis, size, mask):
    return lax.ppermute(x, axis, [(k, k ^ mask) for k in range(size)])


def rotate_kernel(n_parts, cuts, order_ref, *refs):
    x_ref, parts, outs = refs[0], refs[1 : 1 + n_parts], refs[1 + n_parts :]
    basis = jnp.concatenate([part[...] for part in parts], axis=1) if n_parts > 1 else parts[0][...]
    value = jnp.dot(x_ref[...], basis, preferred_element_type=jnp.float32)
    for out, (start, rows) in zip(outs, cuts):
        out[0] = value[start : start + rows]


def rotate(x, basis, me, order_mp, order_dp, cuts):
    rows, feats = x.shape
    n_mp, n_dp = len(order_mp), len(order_dp[1])
    width = basis.shape[1] // n_mp
    cell = width // n_dp
    blocks = me ^ jnp.array(order_mp, jnp.int32)
    cells = order_dp[0] ^ jnp.array(order_dp[1], jnp.int32)
    if cell % LANES:
        chosen = jnp.take(jnp.take(basis.reshape(feats, n_mp, n_dp, cell), blocks, axis=1), cells, axis=2)
        value = jnp.einsum("rf,fpec->prec", x, chosen, preferred_element_type=jnp.float32)
        value = value.reshape(n_mp, rows, width)
        return [value[:, start : start + size] for start, size in cuts]
    order = jnp.concatenate([blocks, cells])

    def part_map(e, p, order_ref):
        return (0, order_ref[p] * n_dp + order_ref[n_mp + e])

    return pl.pallas_call(
        functools.partial(rotate_kernel, n_dp, tuple(cuts)),
        grid_spec=pltpu.PrefetchScalarGridSpec(
            num_scalar_prefetch=1,
            grid=(n_mp,),
            in_specs=[pl.BlockSpec((rows, feats), lambda p, order_ref: (0, 0))]
            + [pl.BlockSpec((feats, cell), functools.partial(part_map, e)) for e in range(n_dp)],
            out_specs=[pl.BlockSpec((1, size, width), lambda p, order_ref: (p, 0, 0)) for _, size in cuts],
        ),
        out_shape=[jax.ShapeDtypeStruct((n_mp, size, width), jnp.float32) for _, size in cuts],
        name="rotate",
    )(order, x, *([basis] * n_dp))


def reduce_over_mp(parts, gain, n_mp):
    have = parts
    bit = 1
    while bit < n_mp:
        half = have.shape[0] // 2
        got = swap(encode(have[half:], gain), "mp", n_mp, bit)
        have = have[:half] + decode(got, gain)
        bit *= 2
    return have[0].astype(jnp.bfloat16)


def scale_kernel(n_dp, seqs, order_ref, low_ref, high_ref, *refs):
    g_refs, eig_ref, scaled_ref, energy_ref = refs[:n_dp], refs[n_dp], refs[n_dp + 1], refs[n_dp + 2]
    p, half = pl.program_id(0), pl.num_programs(0) // 2

    @pl.when(p == 0)
    def _():
        energy_ref[...] = jnp.zeros_like(energy_ref)

    inverse = 1.0 / (eig_ref[...].astype(jnp.float32) + damping)
    for e in range(n_dp):
        for s in range(seqs):
            span = slice(s * SEQ, (s + 1) * SEQ)
            a = jnp.where(p < half, low_ref[0, e, span, :], high_ref[0, e, span, :])
            outer = lax.dot_general(a, g_refs[e][span, :], (((0,), (0,)), ((), ())), preferred_element_type=jnp.float32)
            n = order_ref[e] * seqs + s
            scaled_ref[n] = (outer * inverse).astype(jnp.bfloat16)
            squares = jnp.sum((outer * outer).reshape(-1, 8, outer.shape[1]), axis=0)
            energy_ref[n] += squares


def scale(low, high, train_g, eig_rows, n_mp, order):
    n_dp, rows, cell = low.shape[1:]
    width = train_g[0].shape[1]
    seqs = rows // SEQ
    total = n_dp * seqs
    half = n_mp // 2
    eig, eig_map = eig_rows
    return pl.pallas_call(
        functools.partial(scale_kernel, n_dp, seqs),
        grid_spec=pltpu.PrefetchScalarGridSpec(
            num_scalar_prefetch=1,
            grid=(n_mp,),
            in_specs=[
                pl.BlockSpec((1, n_dp, rows, cell), lambda p, o: (jnp.minimum(p, half - 1), 0, 0, 0)),
                pl.BlockSpec((1, n_dp, rows, cell), lambda p, o: (jnp.maximum(p - half, 0), 0, 0, 0)),
            ]
            + [pl.BlockSpec((rows, width), lambda p, o: (0, 0)) for _ in range(n_dp)]
            + [pl.BlockSpec((cell, width), eig_map)],
            out_specs=[
                pl.BlockSpec((total, cell, width), lambda p, o: (0, p, 0)),
                pl.BlockSpec((total, 8, width), lambda p, o: (0, 0, 0)),
            ],
        ),
        out_shape=[
            jax.ShapeDtypeStruct((total, n_mp * cell, width), jnp.bfloat16),
            jax.ShapeDtypeStruct((total, 8, width), jnp.float32),
        ],
        name="scale",
    )(order, low, high, *train_g, eig)


def score_kernel(n_dp, seqs, order_ref, low_ref, high_ref, *refs):
    g_refs, scaled_ref, out_ref, a_scr, g_scr = refs[:n_dp], refs[n_dp], refs[n_dp + 1], refs[n_dp + 2], refs[n_dp + 3]
    half, _, rows, cell = low_ref.shape

    @pl.when(pl.program_id(0) == 0)
    def _():
        for e in range(n_dp):
            at = pl.ds(pl.multiple_of(order_ref[e] * rows, rows), rows)
            for p in range(half):
                a_scr[at, p * cell : (p + 1) * cell] = low_ref[p, e]
                a_scr[at, (half + p) * cell : (half + p + 1) * cell] = high_ref[p, e]
            g_scr[at, :] = g_refs[e][...]

    tokens = a_scr.shape[0]
    tile = math.gcd(tokens, 256)
    for t in range(tokens // tile):
        span = slice(t * tile, (t + 1) * tile)
        applied = jnp.dot(a_scr[span, :], scaled_ref[0], preferred_element_type=jnp.float32)
        product = applied * g_scr[span, :].astype(jnp.float32)
        for q in range(tile // SEQ):
            out_ref[0, pl.ds(t * (tile // SEQ) + q, 1), :] = jnp.sum(product[q * SEQ : (q + 1) * SEQ], axis=0, keepdims=True)


def score(low, high, query_g, scaled, chunk, rows, order):
    half, n_dp, _, cell = low.shape
    total, depth, width = scaled.shape
    seqs = rows // SEQ
    return pl.pallas_call(
        functools.partial(score_kernel, n_dp, seqs),
        grid_spec=pltpu.PrefetchScalarGridSpec(
            num_scalar_prefetch=1,
            grid=(total,),
            in_specs=[pl.BlockSpec((half, n_dp, rows, cell), lambda n, o: (0, 0, chunk, 0))] * 2
            + [pl.BlockSpec((rows, width), lambda n, o: (0, 0)) for _ in range(n_dp)]
            + [pl.BlockSpec((1, depth, width), lambda n, o: (n, 0, 0))],
            out_specs=pl.BlockSpec((1, n_dp * seqs, width), lambda n, o: (n, 0, 0)),
            scratch_shapes=[
                pltpu.VMEM((n_dp * rows, depth), jnp.bfloat16),
                pltpu.VMEM((n_dp * rows, width), jnp.bfloat16),
            ],
        ),
        out_shape=jax.ShapeDtypeStruct((total, n_dp * seqs, width), jnp.float32),
        name="score",
    )(order, low, high, *query_g, scaled)


def on_device(n_dp, n_mp, train_acts, train_grads, query_acts, query_grads, basis_in, basis_out, eigvals):
    me, home = lax.axis_index("mp"), lax.axis_index("dp")
    bits = n_mp.bit_length() - 1
    order_mp = [reversed_bits(p, bits) for p in range(n_mp)]
    order_e = list(range(n_dp))
    n_train, n_query = train_acts.shape[0], query_acts.shape[0]
    features, hidden = basis_in.shape[1], basis_out.shape[1]
    cell = features // (n_mp * n_dp)
    width = hidden // n_mp
    gain_a = gain_of(features * ACTS_MAX * BASIS_IN_MAX)
    gain_g = gain_of(hidden * GRADS_MAX * BASIS_OUT_MAX)
    chunks = Q_CHUNKS if n_query % (Q_CHUNKS * SEQ) == 0 else 1
    rows_q = n_query // chunks
    natural = home ^ jnp.arange(n_dp, dtype=jnp.int32)

    acts = jnp.concatenate([train_acts, query_acts], axis=0)
    grads = jnp.concatenate([train_grads, query_grads], axis=0)

    cuts_a = [(0, n_train), (n_train, n_query)]
    parts_a = rotate(acts, basis_in, me, order_mp, (home, order_e), cuts_a)
    cuts_g = [(0, n_train)] + [(n_train + k * rows_q, rows_q) for k in range(chunks)]
    parts_g = rotate(grads, basis_out, me, order_mp, (0, [0]), cuts_g)

    def gathered_a(parts):
        mine = reduce_over_mp(parts, gain_a, n_mp)
        pieces = [mine[:, e * cell : (e + 1) * cell] for e in range(n_dp)]
        pieces = [pieces[0]] + [swap(pieces[e], "dp", n_dp, e) for e in range(1, n_dp)]
        have = jnp.stack(pieces)[None]
        bit = n_mp // 2
        while bit > 1:
            have = jnp.concatenate([have, swap(have, "mp", n_mp, bit)], axis=0)
            bit //= 2
        return have, swap(have, "mp", n_mp, 1)

    def gathered_g(parts):
        mine = reduce_over_mp(parts, gain_g, n_mp)
        return [mine] + [swap(mine, "dp", n_dp, e) for e in range(1, n_dp)]

    train_a = gathered_a(parts_a[0])
    train_g = gathered_g(parts_g[0])
    query_a = gathered_a(parts_a[1])
    query_g = [gathered_g(part) for part in parts_g[1:]]

    order = jnp.concatenate([natural, me ^ jnp.array(order_mp, jnp.int32), home[None].astype(jnp.int32)])

    def eig_map(p, o):
        return (o[n_dp + p] * n_dp + o[n_dp + n_mp], 0)

    scaled, energy = scale(*train_a, train_g, (eigvals, eig_map), n_mp, order)
    total = scaled.shape[0]
    lanes = []
    for k in range(chunks):
        part = jnp.sum(score(*query_a, query_g[k], scaled, k, rows_q, order), axis=2)
        lanes.append(part.reshape(total, n_dp, rows_q // SEQ))
    part = jnp.concatenate(lanes, axis=2).reshape(total, -1)
    sums = jnp.concatenate([part, jnp.sum(energy, axis=(1, 2))[:, None]], axis=1)
    for axis, size in (("mp", n_mp), ("dp", n_dp)):
        bit = 1
        while bit < size:
            sums = sums + swap(sums, axis, size, bit)
            bit *= 2
    own = lax.dynamic_slice_in_dim(sums, home * (total // n_dp), total // n_dp, 0)
    scores = jnp.transpose(own[:, :-1]) * (1.0 / math.sqrt(features * hidden))
    energies = own[:, -1] / (features * hidden)
    return scores, energies


def solution(mesh):
    return jax.shard_map(
        functools.partial(on_device, mesh.shape["dp"], mesh.shape["mp"]),
        mesh=mesh,
        in_specs=(
            P("dp", "mp"),
            P("dp", "mp"),
            P("dp", "mp"),
            P("dp", "mp"),
            P("mp", None),
            P("mp", None),
            P(None, "mp"),
        ),
        out_specs=(P(None, "dp"), P("dp")),
        check_vma=False,
    )
```

time: 402 us -> 249 us (0.62)
  blocking collectives: 143 us -> 0 us
  Pallas kernels: 0 us -> 65.3 us
  matrix products: 53.9 us -> 0 us
  waiting for transfers between devices: 164 us -> 112 us
  starting transfers between devices: 0.12 us -> 44.4 us
  between operations: 13.8 us -> 1.16 us
  local copies, waits for them, and re-layouts: 9.22 us -> 1.52 us
  other arithmetic: 17.3 us -> 24 us
    psum x2 -> x0, blocking collectives: 143 us -> none  [the longest x1 127 us: on_device(): lax.psum(jnp.einsum('fc,rf->cr', columns, acts, preferred_element_type=jn...]
    ppermute x0 -> x41, waiting for transfers between devices: none -> 112 us  [swap(): return lax.ppermute(x, axis, [(k, k ^ mask) for k in range(size)])]
    reduce_scatter x1 -> x0, waiting for transfers between devices: 110 us -> none  [on_device(): lax.psum_scatter(jnp.einsum('fc,rf->cr', columns, grads, preferred_elemen...]
    pallas_call x0 -> x5, Pallas kernels: none -> 65.3 us  [the longest x2 29.5 us: score(): pl.pallas_call(functools.partial(score_kernel, n_dp, seqs), grid_spec=plt...]
    all_gather x2 -> x0, waiting for transfers between devices: 54 us -> none  [the longest x1 54 us: on_device(): lax.all_gather(query_a, 'dp', axis=1, tiled=True)]
    dot_general x4 -> x0, matrix products: 53.9 us -> none  [the longest x1 23.9 us: pair_scores(): jnp.einsum('it,nij->ntj', query_a, scaled, preferred_element_type=jnp.flo...]
    ppermute x0 -> x41, starting transfers between devices: none -> 44.4 us  [swap(): return lax.ppermute(x, axis, [(k, k ^ mask) for k in range(size)])]
    add x1 -> x15, other arithmetic: 11.2 us -> 2.49 us  [the longest x10 2.41 us: reduce_over_mp(): have = have[:half] + decode(got, gain)]
  transfers between devices with their start and end apart: 3 -> 41, of which waited for: 2 -> 18; matrix products, arithmetic and copies ran while one was open for 10% -> 7% of each run, Pallas kernels for 0% -> 17%
where the time goes in v1:
time: 249 us; the launch traced here: 248 us
  waiting for transfers between devices  112 us (45%)
  Pallas kernels  65.3 us (26%)
  starting transfers between devices  44.4 us (18%)
  other arithmetic  24 us (10%)
    ppermute x41, waiting for transfers between devices, swap(): return lax.ppermute(x, axis, [(k, k ^ mask) for k in range(size)])  112 us
    ppermute x41, starting transfers between devices, swap(): return lax.ppermute(x, axis, [(k, k ^ mask) for k in range(size)])  44.4 us
    pallas_call x2, Pallas kernels, score(): pl.pallas_call(functools.partial(score_kernel, n_dp, seqs), grid_spec=plt...  29.5 us
    pallas_call x2, Pallas kernels, rotate(): pl.pallas_call(functools.partial(rotate_kernel, n_dp, tuple(cuts)), grid_...  23.7 us
    pallas_call x1, Pallas kernels, scale(): pl.pallas_call(functools.partial(scale_kernel, n_dp, seqs), grid_spec=plt...  12.1 us
    convert_element_type x15, other arithmetic, encode(): return jnp.where(value < 0, -root, root).astype(jnp.float16)  11.2 us
  transfers between devices with their start and end apart: 41, of which 18 were waited for; matrix products, arithmetic and copies ran while one was open for 7% of the time, Pallas kernels for 17%

profile of v1, /device:TPU:0, one launch (start us, length us, event | category | flops | bytes accessed | tf_op | source)
XLA Modules:
  0.0 248.0 jit_solution(4791468993957634790)
XLA Ops:
  1.9 1.8 pad_maximum_fusion.4.refs_0_
  3.7 9.5 %rotate.2 = (f32[8,128,512]{2,1,0:T(8,128)}, f32[8,256,512]{2,1,0:T(8,128)}) custom-call(s32[12]{0:T(128)} %pad_add_fusion.1.order_ref, bf16[384,512]{1,0:T(8,128)(2,1)} %pad_maximum_fusion.4.refs_0_, bf16[512,4096]{1,0:T(8,128)(2,1)} %refs_4_.2, bf16[512,4096]{1,0:T(8,128)(2,1)} %refs_4_.2, bf16[512,4096]{1,0:T(8,128)(2,1)} %refs_4_.2, ...), custom_call_target="tpu_custom_call" | custom-call | tf_op jit(solution)/shard_map/rotate/pallas_call | solution.py:72
  13.2 1.7 fusion.15
  15.4 2.5 %fusion = f16[4,256,512]{2,1,0:T(8,128)(2,1)S(1)} fusion(f32[8,256,512]{2,1,0:T(8,128)} %get-tuple-element.9), kind=kLoop, calls=%fused_computation.8 | loop fusion | flops 3145728 | bytes 3145728 | tf_op jit(solution)/shard_map/convert_element_type | solution.py:28
  18.7 0.9 pad_maximum_fusion.1.refs_0_
  19.6 14.2 %rotate.3 = (f32[8,128,896]{2,1,0:T(8,128)}, f32[8,128,896]{2,1,0:T(8,128)}, f32[8,128,896]{2,1,0:T(8,128)}) custom-call(s32[9]{0:T(128)} %pad_add_fusion.2.order_ref, bf16[384,896]{1,0:T(8,128)(2,1)} %pad_maximum_fusion.1.refs_0_, bf16[896,7168]{1,0:T(8,128)(2,1)} %refs_1_.3), custom_call_target="tpu_custom_call" | custom-call | tf_op jit(solution)/shard_map/rotate/pallas_call | solution.py:72
  33.8 2.5 fusion.9
  37.2 2.7 %collective-permute-start.16 = (f16[2,128,512]{2,1,0:T(8,128)(2,1)S(1)}, f16[2,128,512]{2,1,0:T(8,128)(2,1)S(1)}, u32[]{:S(2)}, u32[]{:S(2)}) collective-permute-start(f16[2,128,512]{2,1,0:T(8,128)(2,1)S(1)} %fusion.31), channel_id=1, source_target_pairs={{0,2},{1,3},{2,0},{3,1},{4,6},{5,7},{6,4},{7,5},{8,10},{9,11},{10,... | collective-permute-start | bytes 786440 | tf_op jit(solution)/shard_map/ppermute | solution.py:44
  39.9 0.8 fusion.6
  41.0 5.9 %collective-permute-done.16 = f16[2,128,512]{2,1,0:T(8,128)(2,1)S(1)} collective-permute-done((f16[2,128,512]{2,1,0:T(8,128)(2,1)S(1)}, f16[2,128,512]{2,1,0:T(8,128)(2,1)S(1)}, u32[]{:S(2)}, u32[]{:S(2)}) %collective-permute-start.16) | collective-permute-done | bytes 262176 | tf_op jit(solution)/shard_map/ppermute | solution.py:44
  47.1 2.8 %collective-permute-start.17 = (f16[1,128,512]{2,1,0:T(8,128)(2,1)S(1)}, f16[1,128,512]{2,1,0:T(8,128)(2,1)S(1)}, u32[]{:S(2)}, u32[]{:S(2)}) collective-permute-start(f16[1,128,512]{2,1,0:T(8,128)(2,1)S(1)} %fusion.46), channel_id=1, source_target_pairs={{0,4},{1,5},{2,6},{3,7},{4,0},{5,1},{6,2},{7,3},{8,12},{9,13},{10,... | collective-permute-start | bytes 393224 | tf_op jit(solution)/shard_map/ppermute | solution.py:44
  50.8 5.3 %collective-permute-done.17 = f16[1,128,512]{2,1,0:T(8,128)(2,1)S(1)} collective-permute-done((f16[1,128,512]{2,1,0:T(8,128)(2,1)S(1)}, f16[1,128,512]{2,1,0:T(8,128)(2,1)S(1)}, u32[]{:S(2)}, u32[]{:S(2)}) %collective-permute-start.17) | collective-permute-done | bytes 131104 | tf_op jit(solution)/shard_map/ppermute | solution.py:44
  56.2 2.4 collective-permute-start.20
  62.6 1.5 collective-permute-start.1
  65.5 3.4 %collective-permute-start.21 = (bf16[1,4,128,128]{3,2,1,0:T(8,128)(2,1)S(1)}, bf16[1,4,128,128]{3,2,1,0:T(8,128)(2,1)S(1)}, u32[]{:S(2)}, u32[]{:S(2)}) collective-permute-start(bf16[1,4,128,128]{3,2,1,0:T(8,128)(2,1)S(1)} %maximum_bitcast_fusion.1), channel_id=1, source_target_pairs={{0,4},{1,5},{2,6},{3,7},{4,0},{5,1},{6,2},{7,3},{8,12},{9,13},{10,... | collective-permute-start | bytes 393224 | tf_op jit(solution)/shard_map/ppermute | solution.py:44
  68.8 22.4 %collective-permute-done.1 = f16[2,256,512]{2,1,0:T(8,128)(2,1)S(1)} collective-permute-done((f16[2,256,512]{2,1,0:T(8,128)(2,1)S(1)}, f16[2,256,512]{2,1,0:T(8,128)(2,1)S(1)}, u32[]{:S(2)}, u32[]{:S(2)}) %collective-permute-start.1) | collective-permute-done | bytes 524320 | tf_op jit(solution)/shard_map/ppermute | solution.py:44
  92.2 4.2 %collective-permute-done.21 = bf16[1,4,128,128]{3,2,1,0:T(8,128)(2,1)S(1)} collective-permute-done((bf16[1,4,128,128]{3,2,1,0:T(8,128)(2,1)S(1)}, bf16[1,4,128,128]{3,2,1,0:T(8,128)(2,1)S(1)}, u32[]{:S(2)}, u32[]{:S(2)}) %collective-permute-start.21) | collective-permute-done | bytes 131104 | tf_op jit(solution)/shard_map/ppermute | solution.py:44
  96.4 4.0 %collective-permute-start.22 = (bf16[2,4,128,128]{3,2,1,0:T(8,128)(2,1)S(1)}, bf16[2,4,128,128]{3,2,1,0:T(8,128)(2,1)S(1)}, u32[]{:S(2)}, u32[]{:S(2)}) collective-permute-start(bf16[2,4,128,128]{3,2,1,0:T(8,128)(2,1)S(1)} %pad_maximum_fusion.5), channel_id=1, source_target_pairs={{0,2},{1,3},{2,0},{3,1},{4,6},{5,7},{6,4},{7,5},{8,10},{9,11},{10,... | collective-permute-start | bytes 786440 | tf_op jit(solution)/shard_map/ppermute | solution.py:44
  100.4 6.0 %collective-permute-done.2 = f16[1,256,512]{2,1,0:T(8,128)(2,1)S(1)} collective-permute-done((f16[1,256,512]{2,1,0:T(8,128)(2,1)S(1)}, f16[1,256,512]{2,1,0:T(8,128)(2,1)S(1)}, u32[]{:S(2)}, u32[]{:S(2)}) %collective-permute-start.2) | collective-permute-done | bytes 262176 | tf_op jit(solution)/shard_map/ppermute | solution.py:44
  106.5 2.5 collective-permute-start.5
  110.1 1.6 collective-permute-done.5
  111.7 1.5 collective-permute-done.4
  114.7 2.5 %collective-permute-start.32 = (f16[1,128,896]{2,1,0:T(8,128)(2,1)S(1)}, f16[1,128,896]{2,1,0:T(8,128)(2,1)S(1)}, u32[]{:S(2)}, u32[]{:S(2)}) collective-permute-start(f16[1,128,896]{2,1,0:T(8,128)(2,1)S(1)} %fusion.42), channel_id=1, source_target_pairs={{0,4},{1,5},{2,6},{3,7},{4,0},{5,1},{6,2},{7,3},{8,12},{9,13},{10,... | collective-permute-start | bytes 688136 | tf_op jit(solution)/shard_map/ppermute | solution.py:44
  117.2 16.8 %collective-permute-done.6 = bf16[1,4,256,128]{3,2,1,0:T(8,128)(2,1)S(1)} collective-permute-done((bf16[1,4,256,128]{3,2,1,0:T(8,128)(2,1)S(1)}, bf16[1,4,256,128]{3,2,1,0:T(8,128)(2,1)S(1)}, u32[]{:S(2)}, u32[]{:S(2)}) %collective-permute-start.6) | collective-permute-done | bytes 262176 | tf_op jit(solution)/shard_map/ppermute | solution.py:44
  134.5 2.1 collective-permute-start.26
  136.8 16.8 %collective-permute-done.7 = bf16[2,4,256,128]{3,2,1,0:T(8,128)(2,1)S(1)} collective-permute-done((bf16[2,4,256,128]{3,2,1,0:T(8,128)(2,1)S(1)}, bf16[2,4,256,128]{3,2,1,0:T(8,128)(2,1)S(1)}, u32[]{:S(2)}, u32[]{:S(2)}) %collective-permute-start.7) | collective-permute-done | bytes 524320 | tf_op jit(solution)/shard_map/ppermute | solution.py:44
  154.3 1.7 collective-permute-start.28
  156.0 10.9 %collective-permute-done.11 = f16[1,128,896]{2,1,0:T(8,128)(2,1)S(1)} collective-permute-done((f16[1,128,896]{2,1,0:T(8,128)(2,1)S(1)}, f16[1,128,896]{2,1,0:T(8,128)(2,1)S(1)}, u32[]{:S(2)}, u32[]{:S(2)}) %collective-permute-start.11) | collective-permute-done | bytes 229408 | tf_op jit(solution)/shard_map/ppermute | solution.py:44
  167.4 3.2 %collective-permute-start.13 = (bf16[128,896]{1,0:T(8,128)(2,1)S(1)}, bf16[128,896]{1,0:T(8,128)(2,1)S(1)}, u32[]{:S(2)}, u32[]{:S(2)}) collective-permute-start(bf16[128,896]{1,0:T(8,128)(2,1)S(1)} %fusion.53.refs_0_), channel_id=1, source_target_pairs={{0,16},{8,24},{16,0},{24,8},{1,17},{9,25},{17,1},{25,9},{2,18},{10... | collective-permute-start | bytes 688136 | tf_op jit(solution)/shard_map/ppermute | solution.py:44
  170.6 4.8 %collective-permute-done.27.refs_1_ = bf16[128,896]{1,0:T(8,128)(2,1)S(1)} collective-permute-done((bf16[128,896]{1,0:T(8,128)(2,1)S(1)}, bf16[128,896]{1,0:T(8,128)(2,1)S(1)}, u32[]{:S(2)}, u32[]{:S(2)}) %collective-permute-start.27) | collective-permute-done | bytes 229408 | tf_op jit(solution)/shard_map/ppermute | solution.py:44
  175.7 2.4 collective-permute-done.14.refs_3_
  178.1 3.4 %collective-permute-start.35 = (bf16[128,896]{1,0:T(8,128)(2,1)S(1)}, bf16[128,896]{1,0:T(8,128)(2,1)}, u32[]{:S(2)}, u32[]{:S(2)}) collective-permute-start(bf16[128,896]{1,0:T(8,128)(2,1)S(1)} %fusion.51.refs_0_), channel_id=1, source_target_pairs={{0,24},{8,16},{16,8},{24,0},{1,25},{9,17},{17,9},{25,1},{2,26},{10... | collective-permute-start | bytes 688136 | tf_op jit(solution)/shard_map/ppermute | solution.py:44
  181.5 1.0 collective-permute-start.34
  182.5 0.8 collective-permute-start.33
  183.9 12.1 %scale.1 = (bf16[8,1024,896]{2,1,0:T(8,128)(2,1)}, f32[8,8,896]{2,1,0:T(8,128)}) custom-call(s32[13]{0:T(128)} %pad_add_fusion.order_ref, bf16[4,4,128,128]{3,2,1,0:T(8,128)(2,1)} %copy-done.6, bf16[4,4,128,128]{3,2,1,0:T(8,128)(2,1)} %copy-done.11, bf16[128,896]{1,0:T(8,128)(2,1)} %copy-done.8, bf16[128,896]{1,0:T(8,128)(2,1)} %copy-done.16, ...), custom_call_target="tpu_custom_call" | custom-call | tf_op jit(solution)/shard_map/scale/pallas_call | solution.py:124
  196.1 1.1 reduce_sum.29
  197.3 1.0 copy-done.2
  198.3 14.7 %score.2 = f32[8,8,896]{2,1,0:T(8,128)} custom-call(s32[13]{0:T(128)} %pad_add_fusion.order_ref, bf16[4,4,256,128]{3,2,1,0:T(8,128)(2,1)} %copy-done, bf16[4,4,256,128]{3,2,1,0:T(8,128)(2,1)} %copy-done.2, bf16[128,896]{1,0:T(8,128)(2,1)} %copy-done.9, bf16[128,896]{1,0:T(8,128)(2,1)} %collective-permute-done.12.refs_1_, bf16[128,896]{1,0:T(8,128)(2,1)} %copy-done.18, ...), custom_call_target="tpu_custom_call" | custom-call | tf_op jit(solution)/shard_map/score/pallas_call | solution.py:175
  213.0 1.0 reduce_sum.27
  214.1 14.7 %score.3 = f32[8,8,896]{2,1,0:T(8,128)} custom-call(s32[13]{0:T(128)} %pad_add_fusion.order_ref, bf16[4,4,256,128]{3,2,1,0:T(8,128)(2,1)} %copy-done, bf16[4,4,256,128]{3,2,1,0:T(8,128)(2,1)} %copy-done.2, bf16[128,896]{1,0:T(8,128)(2,1)} %copy-done.10, bf16[128,896]{1,0:T(8,128)(2,1)} %collective-permute-done.33.refs_1_, ...), custom_call_target="tpu_custom_call" | custom-call | tf_op jit(solution)/shard_map/score/pallas_call | solution.py:175
  228.8 1.0 reduce_sum.28
  230.1 1.2 collective-permute-done.36
  231.4 3.6 %collective-permute-done.37 = f32[8,17]{1,0:T(8,128)S(1)} collective-permute-done((f32[8,17]{1,0:T(8,128)S(1)}, f32[8,17]{1,0:T(8,128)S(1)}, u32[]{:S(2)}, u32[]{:S(2)}) %collective-permute-start.37) | collective-permute-done | bytes 576 | tf_op jit(solution)/shard_map/ppermute | solution.py:44
  235.7 3.8 %collective-permute-done.38 = f32[8,17]{1,0:T(8,128)S(1)} collective-permute-done((f32[8,17]{1,0:T(8,128)S(1)}, f32[8,17]{1,0:T(8,128)S(1)}, u32[]{:S(2)}, u32[]{:S(2)}) %collective-permute-start.38) | collective-permute-done | bytes 576 | tf_op jit(solution)/shard_map/ppermute | solution.py:44
  239.5 1.2 collective-permute-start.39
  240.7 2.4 collective-permute-done.39
  243.1 1.9 collective-permute-start.40
  245.1 1.7 collective-permute-done.40
  (139 shorter events, 19.1 us)
Async XLA Ops:
  14.9 21.9 %collective-permute-start.15 = (f16[4,128,512]{2,1,0:T(8,128)(2,1)S(1)}, f16[4,128,512]{2,1,0:T(8,128)(2,1)S(1)}, u32[]{:S(2)}, u32[]{:S(2)}) collective-permute-start(f16[4,128,512]{2,1,0:T(8,128)(2,1)S(1)} %fusion.15), channel_id=1, source_target_pairs={{0,1},{1,0},{2,3},{3,2},{4,5},{5,4},{6,7},{7,6},{8,9},{9,8},{10,11... | collective-permute-start | bytes 1572872 | tf_op jit(solution)/shard_map/ppermute | solution.py:44
  17.9 43.0 %collective-permute-start = (f16[4,256,512]{2,1,0:T(8,128)(2,1)S(1)}, f16[4,256,512]{2,1,0:T(8,128)(2,1)S(1)}, u32[]{:S(2)}, u32[]{:S(2)}) collective-permute-start(f16[4,256,512]{2,1,0:T(8,128)(2,1)S(1)} %fusion), channel_id=1, source_target_pairs={{0,1},{1,0},{2,3},{3,2},{4,5},{5,4},{6,7},{7,6},{8,9},{9,8},{10,11... | collective-permute-start | bytes 3145736 | tf_op jit(solution)/shard_map/ppermute | solution.py:44
  36.3 22.3 %collective-permute-start.30 = (f16[4,128,896]{2,1,0:T(8,128)(2,1)S(1)}, f16[4,128,896]{2,1,0:T(8,128)(2,1)S(1)}, u32[]{:S(2)}, u32[]{:S(2)}) collective-permute-start(f16[4,128,896]{2,1,0:T(8,128)(2,1)S(1)} %fusion.9), channel_id=1, source_target_pairs={{0,1},{1,0},{2,3},{3,2},{4,5},{5,4},{6,7},{7,6},{8,9},{9,8},{10,11... | collective-permute-start | bytes 2752520 | tf_op jit(solution)/shard_map/ppermute | solution.py:44
  37.2 9.6 %collective-permute-start.16 = (f16[2,128,512]{2,1,0:T(8,128)(2,1)S(1)}, f16[2,128,512]{2,1,0:T(8,128)(2,1)S(1)}, u32[]{:S(2)}, u32[]{:S(2)}) collective-permute-start(f16[2,128,512]{2,1,0:T(8,128)(2,1)S(1)} %fusion.31), channel_id=1, source_target_pairs={{0,2},{1,3},{2,0},{3,1},{4,6},{5,7},{6,4},{7,5},{8,10},{9,11},{10,... | collective-permute-start | bytes 786440 | tf_op jit(solution)/shard_map/ppermute | solution.py:44
  40.8 18.7 %collective-permute-start.24 = (f16[4,128,896]{2,1,0:T(8,128)(2,1)S(1)}, f16[4,128,896]{2,1,0:T(8,128)(2,1)S(1)}, u32[]{:S(2)}, u32[]{:S(2)}) collective-permute-start(f16[4,128,896]{2,1,0:T(8,128)(2,1)S(1)} %fusion.6), channel_id=1, source_target_pairs={{0,1},{1,0},{2,3},{3,2},{4,5},{5,4},{6,7},{7,6},{8,9},{9,8},{10,11... | collective-permute-start | bytes 2752520 | tf_op jit(solution)/shard_map/ppermute | solution.py:44
  47.1 9.0 %collective-permute-start.17 = (f16[1,128,512]{2,1,0:T(8,128)(2,1)S(1)}, f16[1,128,512]{2,1,0:T(8,128)(2,1)S(1)}, u32[]{:S(2)}, u32[]{:S(2)}) collective-permute-start(f16[1,128,512]{2,1,0:T(8,128)(2,1)S(1)} %fusion.46), channel_id=1, source_target_pairs={{0,4},{1,5},{2,6},{3,7},{4,0},{5,1},{6,2},{7,3},{8,12},{9,13},{10,... | collective-permute-start | bytes 393224 | tf_op jit(solution)/shard_map/ppermute | solution.py:44
  50.7 11.8 %collective-permute-start.9 = (f16[4,128,896]{2,1,0:T(8,128)(2,1)S(1)}, f16[4,128,896]{2,1,0:T(8,128)(2,1)S(1)}, u32[]{:S(2)}, u32[]{:S(2)}) collective-permute-start(f16[4,128,896]{2,1,0:T(8,128)(2,1)S(1)} %fusion.3), channel_id=1, source_target_pairs={{0,1},{1,0},{2,3},{3,2},{4,5},{5,4},{6,7},{7,6},{8,9},{9,8},{10,11... | collective-permute-start | bytes 2752520 | tf_op jit(solution)/shard_map/ppermute | solution.py:44
  56.2 8.5 %collective-permute-start.20 = (bf16[128,128]{1,0:T(8,128)(2,1)S(1)}, bf16[128,128]{1,0:T(8,128)(2,1)S(1)}, u32[]{:S(2)}, u32[]{:S(2)}) collective-permute-start(bf16[128,128]{1,0:T(8,128)(2,1)S(1)} %get-tuple-element.23), channel_id=1, source_target_pairs={{0,24},{8,16},{16,8},{24,0},{1,25},{9,17},{17,9},{25,1},{2,26},{10... | collective-permute-start | bytes 98312 | tf_op jit(solution)/shard_map/ppermute | solution.py:44
  58.6 6.8 %collective-permute-start.19 = (bf16[128,128]{1,0:T(8,128)(2,1)S(1)}, bf16[128,128]{1,0:T(8,128)(2,1)S(1)}, u32[]{:S(2)}, u32[]{:S(2)}) collective-permute-start(bf16[128,128]{1,0:T(8,128)(2,1)S(1)} %get-tuple-element.24), channel_id=1, source_target_pairs={{0,16},{8,24},{16,0},{24,8},{1,17},{9,25},{17,1},{25,9},{2,18},{10... | collective-permute-start | bytes 98312 | tf_op jit(solution)/shard_map/ppermute | solution.py:44
  59.4 6.0 %collective-permute-start.18 = (bf16[128,128]{1,0:T(8,128)(2,1)S(1)}, bf16[128,128]{1,0:T(8,128)(2,1)S(1)}, u32[]{:S(2)}, u32[]{:S(2)}) collective-permute-start(bf16[128,128]{1,0:T(8,128)(2,1)S(1)} %get-tuple-element.25), channel_id=1, source_target_pairs={{0,8},{8,0},{16,24},{24,16},{1,9},{9,1},{17,25},{25,17},{2,10},{10... | collective-permute-start | bytes 98312 | tf_op jit(solution)/shard_map/ppermute | solution.py:44
  60.9 53.4 %collective-permute-start.31 = (f16[2,128,896]{2,1,0:T(8,128)(2,1)S(1)}, f16[2,128,896]{2,1,0:T(8,128)(2,1)S(1)}, u32[]{:S(2)}, u32[]{:S(2)}) collective-permute-start(f16[2,128,896]{2,1,0:T(8,128)(2,1)S(1)} %fusion.24), channel_id=1, source_target_pairs={{0,2},{1,3},{2,0},{3,1},{4,6},{5,7},{6,4},{7,5},{8,10},{9,11},{10,... | collective-permute-start | bytes 1376264 | tf_op jit(solution)/shard_map/ppermute | solution.py:44
  62.6 28.7 %collective-permute-start.1 = (f16[2,256,512]{2,1,0:T(8,128)(2,1)S(1)}, f16[2,256,512]{2,1,0:T(8,128)(2,1)S(1)}, u32[]{:S(2)}, u32[]{:S(2)}) collective-permute-start(f16[2,256,512]{2,1,0:T(8,128)(2,1)S(1)} %fusion.12), channel_id=1, source_target_pairs={{0,2},{1,3},{2,0},{3,1},{4,6},{5,7},{6,4},{7,5},{8,10},{9,11},{10,... | collective-permute-start | bytes 1572872 | tf_op jit(solution)/shard_map/ppermute | solution.py:44
  64.7 69.4 %collective-permute-start.25 = (f16[2,128,896]{2,1,0:T(8,128)(2,1)S(1)}, f16[2,128,896]{2,1,0:T(8,128)(2,1)S(1)}, u32[]{:S(2)}, u32[]{:S(2)}) collective-permute-start(f16[2,128,896]{2,1,0:T(8,128)(2,1)S(1)} %fusion.21), channel_id=1, source_target_pairs={{0,2},{1,3},{2,0},{3,1},{4,6},{5,7},{6,4},{7,5},{8,10},{9,11},{10,... | collective-permute-start | bytes 1376264 | tf_op jit(solution)/shard_map/ppermute | solution.py:44
  65.5 30.9 %collective-permute-start.21 = (bf16[1,4,128,128]{3,2,1,0:T(8,128)(2,1)S(1)}, bf16[1,4,128,128]{3,2,1,0:T(8,128)(2,1)S(1)}, u32[]{:S(2)}, u32[]{:S(2)}) collective-permute-start(bf16[1,4,128,128]{3,2,1,0:T(8,128)(2,1)S(1)} %maximum_bitcast_fusion.1), channel_id=1, source_target_pairs={{0,4},{1,5},{2,6},{3,7},{4,0},{5,1},{6,2},{7,3},{8,12},{9,13},{10,... | collective-permute-start | bytes 393224 | tf_op jit(solution)/shard_map/ppermute | solution.py:44
  91.7 14.7 %collective-permute-start.2 = (f16[1,256,512]{2,1,0:T(8,128)(2,1)S(1)}, f16[1,256,512]{2,1,0:T(8,128)(2,1)S(1)}, u32[]{:S(2)}, u32[]{:S(2)}) collective-permute-start(f16[1,256,512]{2,1,0:T(8,128)(2,1)S(1)} %fusion.27), channel_id=1, source_target_pairs={{0,4},{1,5},{2,6},{3,7},{4,0},{5,1},{6,2},{7,3},{8,12},{9,13},{10,... | collective-permute-start | bytes 786440 | tf_op jit(solution)/shard_map/ppermute | solution.py:44
  96.4 13.1 %collective-permute-start.22 = (bf16[2,4,128,128]{3,2,1,0:T(8,128)(2,1)S(1)}, bf16[2,4,128,128]{3,2,1,0:T(8,128)(2,1)S(1)}, u32[]{:S(2)}, u32[]{:S(2)}) collective-permute-start(bf16[2,4,128,128]{3,2,1,0:T(8,128)(2,1)S(1)} %pad_maximum_fusion.5), channel_id=1, source_target_pairs={{0,2},{1,3},{2,0},{3,1},{4,6},{5,7},{6,4},{7,5},{8,10},{9,11},{10,... | collective-permute-start | bytes 786440 | tf_op jit(solution)/shard_map/ppermute | solution.py:44
  106.5 5.2 %collective-permute-start.5 = (bf16[256,128]{1,0:T(8,128)(2,1)S(1)}, bf16[256,128]{1,0:T(8,128)(2,1)S(1)}, u32[]{:S(2)}, u32[]{:S(2)}) collective-permute-start(bf16[256,128]{1,0:T(8,128)(2,1)S(1)} %get-tuple-element.19), channel_id=1, source_target_pairs={{0,24},{8,16},{16,8},{24,0},{1,25},{9,17},{17,9},{25,1},{2,26},{10... | collective-permute-start | bytes 196616 | tf_op jit(solution)/shard_map/ppermute | solution.py:44
  109.0 4.3 %collective-permute-start.4 = (bf16[256,128]{1,0:T(8,128)(2,1)S(1)}, bf16[256,128]{1,0:T(8,128)(2,1)S(1)}, u32[]{:S(2)}, u32[]{:S(2)}) collective-permute-start(bf16[256,128]{1,0:T(8,128)(2,1)S(1)} %get-tuple-element.20), channel_id=1, source_target_pairs={{0,16},{8,24},{16,0},{24,8},{1,17},{9,25},{17,1},{25,9},{2,18},{10... | collective-permute-start | bytes 196616 | tf_op jit(solution)/shard_map/ppermute | solution.py:44
  109.5 4.3 %collective-permute-start.3 = (bf16[256,128]{1,0:T(8,128)(2,1)S(1)}, bf16[256,128]{1,0:T(8,128)(2,1)S(1)}, u32[]{:S(2)}, u32[]{:S(2)}) collective-permute-start(bf16[256,128]{1,0:T(8,128)(2,1)S(1)} %get-tuple-element.21), channel_id=1, source_target_pairs={{0,8},{8,0},{16,24},{24,16},{1,9},{9,1},{17,25},{25,17},{2,10},{10... | collective-permute-start | bytes 196616 | tf_op jit(solution)/shard_map/ppermute | solution.py:44
  110.1 23.9 %copy-start.6 = (bf16[4,4,128,128]{3,2,1,0:T(8,128)(2,1)}, bf16[4,4,128,128]{3,2,1,0:T(8,128)(2,1)S(1)}, u32[]{:S(2)}) copy-start(bf16[4,4,128,128]{3,2,1,0:T(8,128)(2,1)S(1)} %pad_maximum_fusion.3.low_ref) | copy-start | bytes 1572868
  111.7 24.9 %collective-permute-start.10 = (f16[2,128,896]{2,1,0:T(8,128)(2,1)S(1)}, f16[2,128,896]{2,1,0:T(8,128)(2,1)S(1)}, u32[]{:S(2)}, u32[]{:S(2)}) collective-permute-start(f16[2,128,896]{2,1,0:T(8,128)(2,1)S(1)} %fusion.18), channel_id=1, source_target_pairs={{0,2},{1,3},{2,0},{3,1},{4,6},{5,7},{6,4},{7,5},{8,10},{9,11},{10,... | collective-permute-start | bytes 1376264 | tf_op jit(solution)/shard_map/ppermute | solution.py:44
  113.2 69.3 %collective-permute-start.23 = (bf16[4,4,128,128]{3,2,1,0:T(8,128)(2,1)S(1)}, bf16[4,4,128,128]{3,2,1,0:T(8,128)(2,1)S(1)}, u32[]{:S(2)}, u32[]{:S(2)}) collective-permute-start(bf16[4,4,128,128]{3,2,1,0:T(8,128)(2,1)S(1)} %pad_maximum_fusion.3.low_ref), channel_id=1, source_target_pairs={{0,1},{1,0},{2,3},{3,2},{4,5},{5,4},{6,7},{7,6},{8,9},{9,8},{10,11... | collective-permute-start | bytes 1572872 | tf_op jit(solution)/shard_map/ppermute | solution.py:44
  113.8 20.2 %collective-permute-start.6 = (bf16[1,4,256,128]{3,2,1,0:T(8,128)(2,1)S(1)}, bf16[1,4,256,128]{3,2,1,0:T(8,128)(2,1)S(1)}, u32[]{:S(2)}, u32[]{:S(2)}) collective-permute-start(bf16[1,4,256,128]{3,2,1,0:T(8,128)(2,1)S(1)} %maximum_bitcast_fusion), channel_id=1, source_target_pairs={{0,4},{1,5},{2,6},{3,7},{4,0},{5,1},{6,2},{7,3},{8,12},{9,13},{10,... | collective-permute-start | bytes 786440 | tf_op jit(solution)/shard_map/ppermute | solution.py:44
  114.7 39.6 %collective-permute-start.32 = (f16[1,128,896]{2,1,0:T(8,128)(2,1)S(1)}, f16[1,128,896]{2,1,0:T(8,128)(2,1)S(1)}, u32[]{:S(2)}, u32[]{:S(2)}) collective-permute-start(f16[1,128,896]{2,1,0:T(8,128)(2,1)S(1)} %fusion.42), channel_id=1, source_target_pairs={{0,4},{1,5},{2,6},{3,7},{4,0},{5,1},{6,2},{7,3},{8,12},{9,13},{10,... | collective-permute-start | bytes 688136 | tf_op jit(solution)/shard_map/ppermute | solution.py:44
  134.1 19.5 %collective-permute-start.7 = (bf16[2,4,256,128]{3,2,1,0:T(8,128)(2,1)S(1)}, bf16[2,4,256,128]{3,2,1,0:T(8,128)(2,1)S(1)}, u32[]{:S(2)}, u32[]{:S(2)}) collective-permute-start(bf16[2,4,256,128]{3,2,1,0:T(8,128)(2,1)S(1)} %pad_maximum_fusion.2), channel_id=1, source_target_pairs={{0,2},{1,3},{2,0},{3,1},{4,6},{5,7},{6,4},{7,5},{8,10},{9,11},{10,... | collective-permute-start | bytes 1572872 | tf_op jit(solution)/shard_map/ppermute | solution.py:44
  134.5 19.6 %collective-permute-start.26 = (f16[1,128,896]{2,1,0:T(8,128)(2,1)S(1)}, f16[1,128,896]{2,1,0:T(8,128)(2,1)S(1)}, u32[]{:S(2)}, u32[]{:S(2)}) collective-permute-start(f16[1,128,896]{2,1,0:T(8,128)(2,1)S(1)} %fusion.38), channel_id=1, source_target_pairs={{0,4},{1,5},{2,6},{3,7},{4,0},{5,1},{6,2},{7,3},{8,12},{9,13},{10,... | collective-permute-start | bytes 688136 | tf_op jit(solution)/shard_map/ppermute | solution.py:44
  153.7 42.4 %copy-start = (bf16[4,4,256,128]{3,2,1,0:T(8,128)(2,1)}, bf16[4,4,256,128]{3,2,1,0:T(8,128)(2,1)S(1)}, u32[]{:S(2)}) copy-start(bf16[4,4,256,128]{3,2,1,0:T(8,128)(2,1)S(1)} %pad_maximum_fusion.low_ref) | copy-start | bytes 3145732
  153.7 43.6 %collective-permute-start.8 = (bf16[4,4,256,128]{3,2,1,0:T(8,128)(2,1)S(1)}, bf16[4,4,256,128]{3,2,1,0:T(8,128)(2,1)S(1)}, u32[]{:S(2)}, u32[]{:S(2)}) collective-permute-start(bf16[4,4,256,128]{3,2,1,0:T(8,128)(2,1)S(1)} %pad_maximum_fusion.low_ref), channel_id=1, source_target_pairs={{0,1},{1,0},{2,3},{3,2},{4,5},{5,4},{6,7},{7,6},{8,9},{9,8},{10,11... | collective-permute-start | bytes 3145736 | tf_op jit(solution)/shard_map/ppermute | solution.py:44
  154.0 12.9 %collective-permute-start.11 = (f16[1,128,896]{2,1,0:T(8,128)(2,1)S(1)}, f16[1,128,896]{2,1,0:T(8,128)(2,1)S(1)}, u32[]{:S(2)}, u32[]{:S(2)}) collective-permute-start(f16[1,128,896]{2,1,0:T(8,128)(2,1)S(1)} %fusion.34), channel_id=1, source_target_pairs={{0,4},{1,5},{2,6},{3,7},{4,0},{5,1},{6,2},{7,3},{8,12},{9,13},{10,... | collective-permute-start | bytes 688136 | tf_op jit(solution)/shard_map/ppermute | solution.py:44
  154.2 29.7 %copy-start.8 = (bf16[128,896]{1,0:T(8,128)(2,1)}, bf16[128,896]{1,0:T(8,128)(2,1)S(1)}, u32[]{:S(2)}) copy-start(bf16[128,896]{1,0:T(8,128)(2,1)S(1)} %fusion.52.refs_0_) | copy-start | bytes 688132
  154.2 13.1 %collective-permute-start.29 = (bf16[128,896]{1,0:T(8,128)(2,1)S(1)}, bf16[128,896]{1,0:T(8,128)(2,1)S(1)}, u32[]{:S(2)}, u32[]{:S(2)}) collective-permute-start(bf16[128,896]{1,0:T(8,128)(2,1)S(1)} %fusion.52.refs_0_), channel_id=1, source_target_pairs={{0,24},{8,16},{16,8},{24,0},{1,25},{9,17},{17,9},{25,1},{2,26},{10... | collective-permute-start | bytes 688136 | tf_op jit(solution)/shard_map/ppermute | solution.py:44
  154.3 13.1 %collective-permute-start.28 = (bf16[128,896]{1,0:T(8,128)(2,1)S(1)}, bf16[128,896]{1,0:T(8,128)(2,1)S(1)}, u32[]{:S(2)}, u32[]{:S(2)}) collective-permute-start(bf16[128,896]{1,0:T(8,128)(2,1)S(1)} %fusion.52.refs_0_), channel_id=1, source_target_pairs={{0,16},{8,24},{16,0},{24,8},{1,17},{9,25},{17,1},{25,9},{2,18},{10... | collective-permute-start | bytes 688136 | tf_op jit(solution)/shard_map/ppermute | solution.py:44
  166.9 8.5 %collective-permute-start.27 = (bf16[128,896]{1,0:T(8,128)(2,1)S(1)}, bf16[128,896]{1,0:T(8,128)(2,1)S(1)}, u32[]{:S(2)}, u32[]{:S(2)}) collective-permute-start(bf16[128,896]{1,0:T(8,128)(2,1)S(1)} %fusion.52.refs_0_), channel_id=1, source_target_pairs={{0,8},{8,0},{16,24},{24,16},{1,9},{9,1},{17,25},{25,17},{2,10},{10... | collective-permute-start | bytes 688136 | tf_op jit(solution)/shard_map/ppermute | solution.py:44
  167.3 28.8 %copy-start.9 = (bf16[128,896]{1,0:T(8,128)(2,1)}, bf16[128,896]{1,0:T(8,128)(2,1)S(1)}, u32[]{:S(2)}) copy-start(bf16[128,896]{1,0:T(8,128)(2,1)S(1)} %fusion.53.refs_0_) | copy-start | bytes 688132
  167.3 16.7 %copy-start.14 = (bf16[128,896]{1,0:T(8,128)(2,1)}, bf16[128,896]{1,0:T(8,128)(2,1)S(1)}, u32[]{:S(2)}) copy-start(bf16[128,896]{1,0:T(8,128)(2,1)S(1)} %collective-permute-done.29.refs_3_) | copy-start | bytes 688132
  167.3 10.8 %collective-permute-start.14 = (bf16[128,896]{1,0:T(8,128)(2,1)S(1)}, bf16[128,896]{1,0:T(8,128)(2,1)S(1)}, u32[]{:S(2)}, u32[]{:S(2)}) collective-permute-start(bf16[128,896]{1,0:T(8,128)(2,1)S(1)} %fusion.53.refs_0_), channel_id=1, source_target_pairs={{0,24},{8,16},{16,8},{24,0},{1,25},{9,17},{17,9},{25,1},{2,26},{10... | collective-permute-start | bytes 688136 | tf_op jit(solution)/shard_map/ppermute | solution.py:44
  167.4 15.1 %copy-start.15 = (bf16[128,896]{1,0:T(8,128)(2,1)}, bf16[128,896]{1,0:T(8,128)(2,1)S(1)}, u32[]{:S(2)}) copy-start(bf16[128,896]{1,0:T(8,128)(2,1)S(1)} %collective-permute-done.28.refs_2_) | copy-start | bytes 688132
  167.4 14.1 %collective-permute-start.13 = (bf16[128,896]{1,0:T(8,128)(2,1)S(1)}, bf16[128,896]{1,0:T(8,128)(2,1)S(1)}, u32[]{:S(2)}, u32[]{:S(2)}) collective-permute-start(bf16[128,896]{1,0:T(8,128)(2,1)S(1)} %fusion.53.refs_0_), channel_id=1, source_target_pairs={{0,16},{8,24},{16,0},{24,8},{1,17},{9,25},{17,1},{25,9},{2,18},{10... | collective-permute-start | bytes 688136 | tf_op jit(solution)/shard_map/ppermute | solution.py:44
  175.4 21.9 %collective-permute-start.12 = (bf16[128,896]{1,0:T(8,128)(2,1)S(1)}, bf16[128,896]{1,0:T(8,128)(2,1)}, u32[]{:S(2)}, u32[]{:S(2)}) collective-permute-start(bf16[128,896]{1,0:T(8,128)(2,1)S(1)} %fusion.53.refs_0_), channel_id=1, source_target_pairs={{0,8},{8,0},{16,24},{24,16},{1,9},{9,1},{17,25},{25,17},{2,10},{10... | collective-permute-start | bytes 688136 | tf_op jit(solution)/shard_map/ppermute | solution.py:44
  175.7 20.4 %copy-start.10 = (bf16[128,896]{1,0:T(8,128)(2,1)}, bf16[128,896]{1,0:T(8,128)(2,1)S(1)}, u32[]{:S(2)}) copy-start(bf16[128,896]{1,0:T(8,128)(2,1)S(1)} %fusion.51.refs_0_) | copy-start | bytes 688132
  178.1 35.9 %collective-permute-start.35 = (bf16[128,896]{1,0:T(8,128)(2,1)S(1)}, bf16[128,896]{1,0:T(8,128)(2,1)}, u32[]{:S(2)}, u32[]{:S(2)}) collective-permute-start(bf16[128,896]{1,0:T(8,128)(2,1)S(1)} %fusion.51.refs_0_), channel_id=1, source_target_pairs={{0,24},{8,16},{16,8},{24,0},{1,25},{9,17},{17,9},{25,1},{2,26},{10... | collective-permute-start | bytes 688136 | tf_op jit(solution)/shard_map/ppermute | solution.py:44
  181.5 32.6 %collective-permute-start.34 = (bf16[128,896]{1,0:T(8,128)(2,1)S(1)}, bf16[128,896]{1,0:T(8,128)(2,1)}, u32[]{:S(2)}, u32[]{:S(2)}) collective-permute-start(bf16[128,896]{1,0:T(8,128)(2,1)S(1)} %fusion.51.refs_0_), channel_id=1, source_target_pairs={{0,16},{8,24},{16,0},{24,8},{1,17},{9,25},{17,1},{25,9},{2,18},{10... | collective-permute-start | bytes 688136 | tf_op jit(solution)/shard_map/ppermute | solution.py:44
  182.5 31.6 %collective-permute-start.33 = (bf16[128,896]{1,0:T(8,128)(2,1)S(1)}, bf16[128,896]{1,0:T(8,128)(2,1)}, u32[]{:S(2)}, u32[]{:S(2)}) collective-permute-start(bf16[128,896]{1,0:T(8,128)(2,1)S(1)} %fusion.51.refs_0_), channel_id=1, source_target_pairs={{0,8},{8,0},{16,24},{24,16},{1,9},{9,1},{17,25},{25,17},{2,10},{10... | collective-permute-start | bytes 688136 | tf_op jit(solution)/shard_map/ppermute | solution.py:44
  230.1 1.2 collective-permute-start.36
  231.4 3.6 %collective-permute-start.37 = (f32[8,17]{1,0:T(8,128)S(1)}, f32[8,17]{1,0:T(8,128)S(1)}, u32[]{:S(2)}, u32[]{:S(2)}) collective-permute-start(f32[8,17]{1,0:T(8,128)S(1)} %fusion.55), channel_id=1, source_target_pairs={{0,2},{1,3},{2,0},{3,1},{4,6},{5,7},{6,4},{7,5},{8,10},{9,11},{10,... | collective-permute-start | bytes 1640 | tf_op jit(solution)/shard_map/ppermute | solution.py:44
  235.0 4.5 %collective-permute-start.38 = (f32[8,17]{1,0:T(8,128)S(1)}, f32[8,17]{1,0:T(8,128)S(1)}, u32[]{:S(2)}, u32[]{:S(2)}) collective-permute-start(f32[8,17]{1,0:T(8,128)S(1)} %add.79), channel_id=1, source_target_pairs={{0,4},{1,5},{2,6},{3,7},{4,0},{5,1},{6,2},{7,3},{8,12},{9,13},{10,... | collective-permute-start | bytes 1640 | tf_op jit(solution)/shard_map/ppermute | solution.py:44
  239.5 3.6 %collective-permute-start.39 = (f32[8,17]{1,0:T(8,128)S(1)}, f32[8,17]{1,0:T(8,128)S(1)}, u32[]{:S(2)}, u32[]{:S(2)}) collective-permute-start(f32[8,17]{1,0:T(8,128)S(1)} %add.80), channel_id=1, source_target_pairs={{0,8},{8,0},{16,24},{24,16},{1,9},{9,1},{17,25},{25,17},{2,10},{10... | collective-permute-start | bytes 1640 | tf_op jit(solution)/shard_map/ppermute | solution.py:44
  243.1 3.6 %collective-permute-start.40 = (f32[8,17]{1,0:T(8,128)S(1)}, f32[8,17]{1,0:T(8,128)S(1)}, u32[]{:S(2)}, u32[]{:S(2)}) collective-permute-start(f32[8,17]{1,0:T(8,128)S(1)} %add.81), channel_id=1, source_target_pairs={{0,16},{8,24},{16,0},{24,8},{1,17},{9,25},{17,1},{25,9},{2,18},{10... | collective-permute-start | bytes 1640 | tf_op jit(solution)/shard_map/ppermute | solution.py:44
  (12 other events, 58.6 us)
